TPU v7x, 128 devices: a whole 4x4x4 slice. The times are simulated.
128 devices in a mesh: dec: 4 (over x_lo, core), ra: 32 (over x_hi, y, z).
Axes of the slice: x: 4 (x_hi: 2, x_lo: 2; x = x_hi * 2 + x_lo), y: 4, z: 4, core: 2. Of those that a mesh axis runs over, the one named last changes fastest.
Arguments:
- params: float32 [128, 44, 384], P(('dec', 'ra')), may hold values from -6 to 6
- mixing: float32 [44, 256], replicated, may hold values from -0.875 to 0.875
- basis: bfloat16 [256, 4096], replicated, may hold values from -0.375 to 0.375
- blend: float32 [128, 4, 64, 64], P(('dec', 'ra')), may hold values from -0.375 to 0.375
- border_ids: int32 [128, 64], P(('dec', 'ra')), may hold values from 0 to 383, as said below
- intersection: int32 [128, 384, 4], P(('dec', 'ra')), may hold values from 0 to 4, all different within a row; in each aligned block of 384 rows (0 to 383, 384 to 767, ..., all dimensions but the last counted through in order) at most 384 rows name the same one
- observed: bfloat16 [128, 5, 384, 4096], P(('dec', 'ra')), may hold values from -6 to 6
Outputs:
- gradient: float32 [128, 44, 384], P(('dec', 'ra'))
Inputs may be any that keep to these rules, and one draw needn't show every extreme that they name: `intersection`: each source names 4 different offset indices; among the sources of one tile each index is named at most 384 times, and exactly 384 times in some tile. `border_ids`: 64 different sources of the tile.
All inputs are finite; a program needn't handle non-finite values.
Results may differ from a plain program's by a relative error of at most 0.0017.
Values may be sent and summed in bfloat16 or wider, within the bound.
A program may use at most 64 MiB of HBM per device.

v0:
```python
import math

import jax
import jax.numpy as jnp
from jax import lax
from jax.sharding import PartitionSpec as P

HIGHEST_PREC = lax.Precision.HIGHEST


def with_halo(block, sides, width):
    for axis, dim in sides:
        count = lax.axis_size(axis)
        forward = [(i, i + 1) for i in range(count - 1)]
        forward.append((count - 1, 0))
        backward = [(target, source) for source, target in forward]
        low = lax.ppermute(
            lax.slice_in_dim(block, block.shape[dim] - width, None, axis=dim), axis, forward
        )
        high = lax.ppermute(lax.slice_in_dim(block, 0, width, axis=dim), axis, backward)
        block = jnp.concatenate([low, block, high], axis=dim)
    return block


def from_behind(shard, axis, by):
    size = lax.axis_size(axis)
    return lax.ppermute(shard, axis, [(i, (i + by) % size) for i in range(size)])


def passed_along(value, axis, steps):
    count = lax.axis_size(axis)
    initial, last = (max(0, -steps), min(count, count - steps))
    return lax.ppermute(value, axis, [(source, source + steps) for source in range(initial, last)])


def render_block(packed, seen, basis, factor):
    rendered = jnp.dot(packed, basis, preferred_element_type=jnp.float32)
    residual = (rendered - seen.astype(jnp.float32)).astype(jnp.bfloat16)
    pulled = lax.dot_general(
        residual, basis, (((1,), (1,)), ((), ())), preferred_element_type=jnp.float32
    )
    return (pulled * factor).astype(jnp.bfloat16)


def local(params, mixing, basis, blend, border_ids, intersection, observed):
    local_params = params[0]
    rim_rows = border_ids[0]
    weights = blend[0]
    seen_all = observed[0]
    offsets = seen_all.shape[0]
    capacity = seen_all.shape[1]
    reach_ra = offsets // 2
    intersections = intersection.shape[2]
    src_count = local_params.shape[1]
    width_k = mixing.shape[1]
    factor = 1.0 / math.sqrt(basis.shape[1])
    dec_size = lax.axis_size("dec")
    dec_index = lax.axis_index("dec")
    logits = jnp.einsum("ps,pk->sk", local_params, mixing, precision=HIGHEST_PREC)
    amplitudes = jax.nn.softplus(logits)
    padded = with_halo(amplitudes[rim_rows][None, None], (("dec", 0), ("ra", 1)), 1)
    from_below = padded[0, 1]
    from_above = padded[2, 1]
    from_west = padded[1, 0]
    from_east = padded[1, 2]
    from_below = jnp.where(dec_index > 0, from_below, 0.0)
    from_above = jnp.where(dec_index < dec_size - 1, from_above, 0.0)
    nearby = jnp.stack([from_below, from_above, from_west, from_east], axis=0)
    light_in = jnp.einsum("sij,sjk->ik", weights, nearby, precision=HIGHEST_PREC)
    blended = amplitudes.at[rim_rows].add(light_in)
    sent_amps = blended.astype(jnp.bfloat16)
    flat_owner = intersection[0].reshape(-1)
    onehot = (flat_owner[:, None] == jnp.arange(offsets, dtype=jnp.int32)[None, :]).astype(
        jnp.int32
    )
    before = jnp.cumsum(onehot, axis=0) - onehot
    slot_index = jnp.sum(onehot * before, axis=1)
    dest_row = flat_owner * capacity + slot_index
    source_row = jnp.arange(flat_owner.shape[0], dtype=jnp.int32) // intersections
    packets = (
        jnp.zeros((offsets * capacity, width_k), jnp.bfloat16)
        .at[dest_row]
        .set(sent_amps[source_row])
    )
    packets = packets.reshape(offsets, capacity, width_k)
    answers = []
    for offset_id in range(offsets):
        step_by = offset_id - reach_ra
        if step_by == 0:
            piece_in = packets[offset_id]
        else:
            piece_in = from_behind(packets[offset_id], "ra", step_by)
        answer = render_block(piece_in, seen_all[offset_id], basis, factor)
        if step_by != 0:
            answer = from_behind(answer, "ra", -step_by)
        answers.append(answer)
    returned = jnp.stack(answers, axis=0)
    gathered = returned.reshape(offsets * capacity, width_k)[dest_row].astype(jnp.float32)
    grad_sent = jnp.sum(gathered.reshape(src_count, intersections, width_k), axis=1)
    rim_grad = grad_sent[rim_rows]
    toward = jnp.einsum("sij,ik->sjk", weights, rim_grad, precision=HIGHEST_PREC)
    incoming = jnp.zeros_like(rim_grad)
    for side_id, step_by in ((0, -1), (1, 1)):
        incoming = incoming + passed_along(toward[side_id], "dec", step_by)
    for side_id, step_by in ((2, -1), (3, 1)):
        incoming = incoming + from_behind(toward[side_id], "ra", step_by)
    grad_amps = grad_sent.at[rim_rows].add(incoming)
    gradient = jnp.einsum(
        "pk,sk->ps", mixing, grad_amps * jax.nn.sigmoid(logits), precision=HIGHEST_PREC
    )
    return gradient[None]


def solution(mesh):
    in_specs = (
        P(("dec", "ra"), None, None),
        P(),
        P(),
        P(("dec", "ra"), None, None, None),
        P(("dec", "ra"), None),
        P(("dec", "ra"), None, None),
        P(("dec", "ra"), None, None, None),
    )
    out_specs = P(("dec", "ra"), None, None)
    return jax.shard_map(local, mesh=mesh, in_specs=in_specs, out_specs=out_specs, check_vma=False)
```

profile of v0, /device:TPU:0, one launch (start us, length us, event | category | flops | bytes accessed | tf_op | source)
XLA Modules:
  0.0 136.4 jit_solution(1120834159169153755)
XLA Ops:
  0.8 2.3 %compare_select_fusion = (f32[384,256]{1,0:T(8,128)S(1)}, f32[384,256]{1,0:T(8,128)}) fusion(f32[44,256]{1,0:T(8,128)} %param.8, f32[1,44,384]{2,0,1:T(1,128)} %param.7), kind=kOutput, calls=%fused_computation.22 | convolution fusion | flops 52494336 | bytes 899072 | tf_op jit(solution)/shard_map/ps,pk->sk/dot_general | solution.py:59
  3.9 1.7 %collective-permute-start.1 = (f32[1,1,64,256]{3,2,1,0:T(8,128)S(1)}, f32[1,1,64,256]{3,2,1,0:T(8,128)S(1)}, u32[]{:S(2)}, u32[]{:S(2)}) collective-permute-start(f32[1,1,64,256]{3,2,1,0:T(8,128)S(1)} %bitcast.122), channel_id=1, source_target_pairs={{32,0},{64,32},{96,64},{0,96},{33,1},{65,33},{97,65},{1,97},{34,2}... | collective-permute-start | bytes 196616 | tf_op jit(solution)/shard_map/ppermute | solution.py:20
  5.6 0.8 copy.11
  7.5 1.4 %reduce-window.6 = s32[5,12,128]{2,1,0:T(8,128)S(1)} reduce-window(s32[5,12,128]{2,1,0:T(8,128)S(1)} %fusion.40, s32[]{:T(128)} %constant.36.clone.1), window={size=1x1x128 pad=0_0x0_0x127_0}, to_apply=%region_0.1 | reduce-window | flops 975360 | bytes 61444 | tf_op jit(solution)/shard_map/reduce-window
  9.9 9.1 %collective-permute-start.3 = (f32[3,1,64,256]{3,2,1,0:T(8,128)S(1)}, f32[3,1,64,256]{3,2,1,0:T(8,128)S(1)}, u32[]{:S(2)}, u32[]{:S(2)}) collective-permute-start(f32[3,1,64,256]{3,2,1,0:T(8,128)S(1)} %pad_maximum_fusion), channel_id=1, source_target_pairs={{1,0},{2,1},{3,2},{4,3},{5,4},{6,5},{7,6},{8,7},{9,8},{10,9},{11,1... | collective-permute-start | bytes 589832 | tf_op jit(solution)/shard_map/ppermute | solution.py:20
  19.0 3.9 %collective-permute-done.3 = f32[3,1,64,256]{3,2,1,0:T(8,128)S(1)} collective-permute-done((f32[3,1,64,256]{3,2,1,0:T(8,128)S(1)}, f32[3,1,64,256]{3,2,1,0:T(8,128)S(1)}, u32[]{:S(2)}, u32[]{:S(2)}) %collective-permute-start.3) | collective-permute-done | bytes 196640 | tf_op jit(solution)/shard_map/ppermute | solution.py:20
  22.9 7.9 %collective-permute-done.2 = f32[3,1,64,256]{3,2,1,0:T(8,128)S(1)} collective-permute-done((f32[3,1,64,256]{3,2,1,0:T(8,128)S(1)}, f32[3,1,64,256]{3,2,1,0:T(8,128)S(1)}, u32[]{:S(2)}, u32[]{:S(2)}) %collective-permute-start.2) | collective-permute-done | bytes 196640 | tf_op jit(solution)/shard_map/ppermute | solution.py:17
  31.1 1.1 scatter_fusion
  32.9 16.9 %scatter_custom_fusion.1 = bf16[1920,256]{1,0:T(8,128)(2,1)S(1)} fusion(s32[1536]{0:T(1024)S(1)} %fusion.41, bf16[384,256]{1,0:T(8,128)(2,1)} %convert_element_type.79, s32[2048]{0:T(1024)S(1)} %pad_clamp_fusion.1, bf16[]{:T(256)} %constant.18.clone.1), kind=kCustom, calls=%fused_computation.32 | custom fusion | bytes 983552 | tf_op jit(solution)/shard_map/scatter | solution.py:83
  49.9 0.9 fusion.47
  51.3 1.7 %collective-permute-start.8 = (bf16[384,256]{1,0:T(8,128)(2,1)}, bf16[384,256]{1,0:T(8,128)(2,1)}, u32[]{:S(2)}, u32[]{:S(2)}) collective-permute-start(bf16[384,256]{1,0:T(8,128)(2,1)} %get-tuple-element.6), channel_id=1, source_target_pairs={{0,1},{1,2},{2,3},{3,4},{4,5},{5,6},{6,7},{7,8},{8,9},{9,10},{10,1... | collective-permute-start | bytes 589832 | tf_op jit(solution)/shard_map/ppermute | solution.py:27
  53.0 3.5 %collective-permute-start.10 = (bf16[384,256]{1,0:T(8,128)(2,1)S(1)}, bf16[384,256]{1,0:T(8,128)(2,1)}, u32[]{:S(2)}, u32[]{:S(2)}) collective-permute-start(bf16[384,256]{1,0:T(8,128)(2,1)S(1)} %get-tuple-element.5), channel_id=1, source_target_pairs={{0,2},{1,3},{2,4},{3,5},{4,6},{5,7},{6,8},{7,9},{8,10},{9,11},{10,... | collective-permute-start | bytes 589832 | tf_op jit(solution)/shard_map/ppermute | solution.py:27
  56.5 11.5 %collective-permute-done.4 = bf16[384,256]{1,0:T(8,128)(2,1)} collective-permute-done((bf16[384,256]{1,0:T(8,128)(2,1)}, bf16[384,256]{1,0:T(8,128)(2,1)}, u32[]{:S(2)}, u32[]{:S(2)}) %collective-permute-start.4) | collective-permute-done | bytes 196640 | tf_op jit(solution)/shard_map/ppermute | solution.py:27
  68.0 4.6 %fusion.5 = bf16[384,256]{1,0:T(8,128)(2,1)} fusion(bf16[256,4096]{1,0:T(8,128)(2,1)S(1)} %copy-done, bf16[384,256]{1,0:T(8,128)(2,1)} %collective-permute-done.4, bf16[1,5,384,4096]{3,2,1,0:T(8,128)(2,1)} %param.13), kind=kOutput, calls=%fused_computation.23 | convolution fusion | flops 1615527936 | bytes 7733248 | tf_op jit(solution)/shard_map/dot_general | solution.py:39
  72.6 4.6 %fusion.6 = bf16[384,256]{1,0:T(8,128)(2,1)} fusion(bf16[256,4096]{1,0:T(8,128)(2,1)S(1)} %copy-done, bf16[384,256]{1,0:T(8,128)(2,1)} %collective-permute-done.6, bf16[1,5,384,4096]{3,2,1,0:T(8,128)(2,1)} %param.13), kind=kOutput, calls=%fused_computation.24 | convolution fusion | flops 1615527936 | bytes 7733248 | tf_op jit(solution)/shard_map/dot_general | solution.py:39
  77.2 4.6 %fusion.8 = bf16[384,256]{1,0:T(8,128)(2,1)} fusion(bf16[256,4096]{1,0:T(8,128)(2,1)S(1)} %copy-done, bf16[384,256]{1,0:T(8,128)(2,1)} %collective-permute-done.8, bf16[1,5,384,4096]{3,2,1,0:T(8,128)(2,1)} %param.13), kind=kOutput, calls=%fused_computation.26 | convolution fusion | flops 1615527936 | bytes 7733248 | tf_op jit(solution)/shard_map/dot_general | solution.py:39
  81.8 7.7 %collective-permute-start.9 = (bf16[384,256]{1,0:T(8,128)(2,1)}, bf16[384,256]{1,0:T(8,128)(2,1)}, u32[]{:S(2)}, u32[]{:S(2)}) collective-permute-start(bf16[384,256]{1,0:T(8,128)(2,1)} %fusion.8), channel_id=1, source_target_pairs={{0,31},{1,0},{2,1},{3,2},{4,3},{5,4},{6,5},{7,6},{8,7},{9,8},{10,9... | collective-permute-start | bytes 589832 | tf_op jit(solution)/shard_map/ppermute | solution.py:27
  89.5 4.6 %fusion.9 = bf16[384,256]{1,0:T(8,128)(2,1)} fusion(bf16[256,4096]{1,0:T(8,128)(2,1)S(1)} %copy-done, bf16[384,256]{1,0:T(8,128)(2,1)} %collective-permute-done.10, bf16[1,5,384,4096]{3,2,1,0:T(8,128)(2,1)} %param.13), kind=kOutput, calls=%fused_computation.27 | convolution fusion | flops 1615527936 | bytes 7733248 | tf_op jit(solution)/shard_map/dot_general | solution.py:39
  94.1 2.3 %collective-permute-start.11 = (bf16[384,256]{1,0:T(8,128)(2,1)}, bf16[384,256]{1,0:T(8,128)(2,1)}, u32[]{:S(2)}, u32[]{:S(2)}) collective-permute-start(bf16[384,256]{1,0:T(8,128)(2,1)} %fusion.9), channel_id=1, source_target_pairs={{0,30},{1,31},{2,0},{3,1},{4,2},{5,3},{6,4},{7,5},{8,6},{9,7},{10,... | collective-permute-start | bytes 589832 | tf_op jit(solution)/shard_map/ppermute | solution.py:27
  96.5 0.9 bitcast_dynamic-update-slice_fusion.3
  97.4 3.9 %fusion.11 = bf16[5,384,256]{2,1,0:T(8,128)(2,1)S(1)} fusion(bf16[5,384,256]{2,1,0:T(8,128)(2,1)S(1)} %bitcast_dynamic-update-slice_fusion.2, bf16[256,4096]{1,0:T(8,128)(2,1)S(1)} %copy-done, bf16[1,5,384,4096]{3,2,1,0:T(8,128)(2,1)} %param.13, bf16[1920,256]{1,0:T(8,128)(2,1)} %copy-done.1), kind=kOutput, calls=%fused_computation.29 | convolution fusion | flops 1615527936 | bytes 7733248 | tf_op jit(solution)/shard_map/dot_general | solution.py:39
  101.4 0.9 bitcast_dynamic-update-slice_fusion.1
  102.3 0.9 bitcast_dynamic-update-slice_fusion
  103.3 5.4 %gather_fusion.1 = bf16[1536,256]{1,0:T(8,128)(2,1)} fusion(bf16[1920,256]{1,0:T(8,128)(2,1)S(1)} %bitcast.118, s32[2048]{0:T(1024)S(1)} %pad_clamp_fusion), kind=kCustom, calls=%fused_computation.2 | custom fusion | bytes 1579008 | tf_op jit(solution)/shard_map/gather | solution.py:98
  108.6 2.6 %reshape.187 = f32[384,4,256]{2,1,0:T(4,128)} reshape(bf16[1536,256]{1,0:T(8,128)(2,1)} %gather_fusion.1) | data formatting | bytes 2359296 | tf_op jit(solution)/shard_map/convert_element_type | solution.py:98
  111.3 2.3 %reduce_sum.22 = f32[384,256]{1,0:T(8,128)S(1)} reduce(f32[384,4,256]{2,1,0:T(4,128)} %reshape.187, f32[]{:T(128)} %constant.38.clone.1), dimensions={1}, to_apply=%region_5.6 | reduce | flops 294912 | bytes 1966084 | tf_op jit(solution)/shard_map/reduce_sum | solution.py:99
  114.8 1.3 collective-permute-start.12
  116.1 3.0 %collective-permute-start.13 = (f32[64,256]{1,0:T(8,128)S(1)}, f32[64,256]{1,0:T(8,128)S(1)}, u32[]{:S(2)}, u32[]{:S(2)}) collective-permute-start(f32[64,256]{1,0:T(8,128)S(1)} %get-tuple-element.9), channel_id=1, source_target_pairs={{0,32},{32,64},{64,96},{1,33},{33,65},{65,97},{2,34},{34,66},{66,9... | collective-permute-start | bytes 196616 | tf_op jit(solution)/shard_map/ppermute | solution.py:33
  119.1 4.7 %collective-permute-start.14 = (f32[64,256]{1,0:T(8,128)S(1)}, f32[64,256]{1,0:T(8,128)S(1)}, u32[]{:S(2)}, u32[]{:S(2)}) collective-permute-start(f32[64,256]{1,0:T(8,128)S(1)} %get-tuple-element.11), channel_id=1, source_target_pairs={{0,31},{1,0},{2,1},{3,2},{4,3},{5,4},{6,5},{7,6},{8,7},{9,8},{10,9... | collective-permute-start | bytes 196616 | tf_op jit(solution)/shard_map/ppermute | solution.py:27
  123.9 1.9 %collective-permute-done.14 = f32[64,256]{1,0:T(8,128)S(1)} collective-permute-done((f32[64,256]{1,0:T(8,128)S(1)}, f32[64,256]{1,0:T(8,128)S(1)}, u32[]{:S(2)}, u32[]{:S(2)}) %collective-permute-start.14) | collective-permute-done | bytes 65568 | tf_op jit(solution)/shard_map/ppermute | solution.py:27
  125.8 8.1 %collective-permute-done.15 = f32[64,256]{1,0:T(8,128)S(1)} collective-permute-done((f32[64,256]{1,0:T(8,128)S(1)}, f32[64,256]{1,0:T(8,128)S(1)}, u32[]{:S(2)}, u32[]{:S(2)}) %collective-permute-start.15) | collective-permute-done | bytes 65568 | tf_op jit(solution)/shard_map/ppermute | solution.py:27
  133.9 1.2 scatter_custom_fusion.2
  (63 shorter events, 7.4 us)
Async XLA Ops:
  0.0 68.0 %copy-start = (bf16[256,4096]{1,0:T(8,128)(2,1)S(1)}, bf16[256,4096]{1,0:T(8,128)(2,1)}, u32[]{:S(2)}) copy-start(bf16[256,4096]{1,0:T(8,128)(2,1)} %param.9) | copy-start | bytes 6291460
  0.0 30.8 %copy-start.3 = (f32[1,4,64,64]{3,2,1,0:T(8,128)S(1)}, f32[1,4,64,64]{3,2,1,0:T(8,128)}, u32[]{:S(2)}) copy-start(f32[1,4,64,64]{3,2,1,0:T(8,128)} %param.10) | copy-start | bytes 196612
  0.8 31.4 %copy-start.6 = (s32[64]{0:T(128)}, s32[64]{0:T(128)S(1)}, u32[]{:S(2)}) copy-start(s32[64]{0:T(128)S(1)} %fusion.43) | copy-start | bytes 772
  0.8 3.0 %copy-start.5 = (s32[1024]{0:T(1024)}, s32[1024]{0:T(1024)S(1)}, u32[]{:S(2)}) copy-start(s32[1024]{0:T(1024)S(1)} %pad_clamp_fusion.2) | copy-start | bytes 12292
  3.8 6.0 %collective-permute-start = (f32[1,1,64,256]{3,2,1,0:T(8,128)S(1)}, f32[1,1,64,256]{3,2,1,0:T(8,128)S(1)}, u32[]{:S(2)}, u32[]{:S(2)}) collective-permute-start(f32[1,1,64,256]{3,2,1,0:T(8,128)S(1)} %bitcast.121), channel_id=1, source_target_pairs={{0,32},{32,64},{64,96},{96,0},{1,33},{33,65},{65,97},{97,1},{2,34}... | collective-permute-start | bytes 196616 | tf_op jit(solution)/shard_map/ppermute | solution.py:17
  3.9 5.9 %collective-permute-start.1 = (f32[1,1,64,256]{3,2,1,0:T(8,128)S(1)}, f32[1,1,64,256]{3,2,1,0:T(8,128)S(1)}, u32[]{:S(2)}, u32[]{:S(2)}) collective-permute-start(f32[1,1,64,256]{3,2,1,0:T(8,128)S(1)} %bitcast.122), channel_id=1, source_target_pairs={{32,0},{64,32},{96,64},{0,96},{33,1},{65,33},{97,65},{1,97},{34,2}... | collective-permute-start | bytes 196616 | tf_op jit(solution)/shard_map/ppermute | solution.py:20
  9.9 13.0 %collective-permute-start.3 = (f32[3,1,64,256]{3,2,1,0:T(8,128)S(1)}, f32[3,1,64,256]{3,2,1,0:T(8,128)S(1)}, u32[]{:S(2)}, u32[]{:S(2)}) collective-permute-start(f32[3,1,64,256]{3,2,1,0:T(8,128)S(1)} %pad_maximum_fusion), channel_id=1, source_target_pairs={{1,0},{2,1},{3,2},{4,3},{5,4},{6,5},{7,6},{8,7},{9,8},{10,9},{11,1... | collective-permute-start | bytes 589832 | tf_op jit(solution)/shard_map/ppermute | solution.py:20
  19.0 11.8 %collective-permute-start.2 = (f32[3,1,64,256]{3,2,1,0:T(8,128)S(1)}, f32[3,1,64,256]{3,2,1,0:T(8,128)S(1)}, u32[]{:S(2)}, u32[]{:S(2)}) collective-permute-start(f32[3,1,64,256]{3,2,1,0:T(8,128)S(1)} %pad_maximum_fusion), channel_id=1, source_target_pairs={{0,1},{1,2},{2,3},{3,4},{4,5},{5,6},{6,7},{7,8},{8,9},{9,10},{10,1... | collective-permute-start | bytes 589832 | tf_op jit(solution)/shard_map/ppermute | solution.py:17
  49.9 22.7 %copy-start.1 = (bf16[1920,256]{1,0:T(8,128)(2,1)}, bf16[1920,256]{1,0:T(8,128)(2,1)S(1)}, u32[]{:S(2)}) copy-start(bf16[1920,256]{1,0:T(8,128)(2,1)S(1)} %scatter_custom_fusion.1) | copy-start | bytes 2949124
  50.8 17.2 %collective-permute-start.4 = (bf16[384,256]{1,0:T(8,128)(2,1)}, bf16[384,256]{1,0:T(8,128)(2,1)}, u32[]{:S(2)}, u32[]{:S(2)}) collective-permute-start(bf16[384,256]{1,0:T(8,128)(2,1)} %get-tuple-element.8), channel_id=1, source_target_pairs={{0,30},{1,31},{2,0},{3,1},{4,2},{5,3},{6,4},{7,5},{8,6},{9,7},{10,... | collective-permute-start | bytes 589832 | tf_op jit(solution)/shard_map/ppermute | solution.py:27
  50.9 21.7 %collective-permute-start.6 = (bf16[384,256]{1,0:T(8,128)(2,1)}, bf16[384,256]{1,0:T(8,128)(2,1)}, u32[]{:S(2)}, u32[]{:S(2)}) collective-permute-start(bf16[384,256]{1,0:T(8,128)(2,1)} %get-tuple-element.7), channel_id=1, source_target_pairs={{0,31},{1,0},{2,1},{3,2},{4,3},{5,4},{6,5},{7,6},{8,7},{9,8},{10,9... | collective-permute-start | bytes 589832 | tf_op jit(solution)/shard_map/ppermute | solution.py:27
  51.3 25.9 %collective-permute-start.8 = (bf16[384,256]{1,0:T(8,128)(2,1)}, bf16[384,256]{1,0:T(8,128)(2,1)}, u32[]{:S(2)}, u32[]{:S(2)}) collective-permute-start(bf16[384,256]{1,0:T(8,128)(2,1)} %get-tuple-element.6), channel_id=1, source_target_pairs={{0,1},{1,2},{2,3},{3,4},{4,5},{5,6},{6,7},{7,8},{8,9},{9,10},{10,1... | collective-permute-start | bytes 589832 | tf_op jit(solution)/shard_map/ppermute | solution.py:27
  53.0 36.6 %collective-permute-start.10 = (bf16[384,256]{1,0:T(8,128)(2,1)S(1)}, bf16[384,256]{1,0:T(8,128)(2,1)}, u32[]{:S(2)}, u32[]{:S(2)}) collective-permute-start(bf16[384,256]{1,0:T(8,128)(2,1)S(1)} %get-tuple-element.5), channel_id=1, source_target_pairs={{0,2},{1,3},{2,4},{3,5},{4,6},{5,7},{6,8},{7,9},{8,10},{9,11},{10,... | collective-permute-start | bytes 589832 | tf_op jit(solution)/shard_map/ppermute | solution.py:27
  72.6 23.9 %collective-permute-start.5 = (bf16[384,256]{1,0:T(8,128)(2,1)}, bf16[384,256]{1,0:T(8,128)(2,1)}, u32[]{:S(2)}, u32[]{:S(2)}) collective-permute-start(bf16[384,256]{1,0:T(8,128)(2,1)} %fusion.5), channel_id=1, source_target_pairs={{0,2},{1,3},{2,4},{3,5},{4,6},{5,7},{6,8},{7,9},{8,10},{9,11},{10,... | collective-permute-start | bytes 589832 | tf_op jit(solution)/shard_map/ppermute | solution.py:27
  77.2 20.2 %collective-permute-start.7 = (bf16[384,256]{1,0:T(8,128)(2,1)}, bf16[384,256]{1,0:T(8,128)(2,1)S(1)}, u32[]{:S(2)}, u32[]{:S(2)}) collective-permute-start(bf16[384,256]{1,0:T(8,128)(2,1)} %fusion.6), channel_id=1, source_target_pairs={{0,1},{1,2},{2,3},{3,4},{4,5},{5,6},{6,7},{7,8},{8,9},{9,10},{10,1... | collective-permute-start | bytes 589832 | tf_op jit(solution)/shard_map/ppermute | solution.py:27
  81.8 19.6 %collective-permute-start.9 = (bf16[384,256]{1,0:T(8,128)(2,1)}, bf16[384,256]{1,0:T(8,128)(2,1)}, u32[]{:S(2)}, u32[]{:S(2)}) collective-permute-start(bf16[384,256]{1,0:T(8,128)(2,1)} %fusion.8), channel_id=1, source_target_pairs={{0,31},{1,0},{2,1},{3,2},{4,3},{5,4},{6,5},{7,6},{8,7},{9,8},{10,9... | collective-permute-start | bytes 589832 | tf_op jit(solution)/shard_map/ppermute | solution.py:27
  94.1 8.2 %collective-permute-start.11 = (bf16[384,256]{1,0:T(8,128)(2,1)}, bf16[384,256]{1,0:T(8,128)(2,1)}, u32[]{:S(2)}, u32[]{:S(2)}) collective-permute-start(bf16[384,256]{1,0:T(8,128)(2,1)} %fusion.9), channel_id=1, source_target_pairs={{0,30},{1,31},{2,0},{3,1},{4,2},{5,3},{6,4},{7,5},{8,6},{9,7},{10,... | collective-permute-start | bytes 589832 | tf_op jit(solution)/shard_map/ppermute | solution.py:27
  108.6 26.5 %copy-start.2 = (f32[384,256]{1,0:T(8,128)S(1)}, f32[384,256]{1,0:T(8,128)}, u32[]{:S(2)}) copy-start(f32[384,256]{1,0:T(8,128)} %get-tuple-element.14) | copy-start | bytes 1179652
  108.6 26.5 %copy-start.4 = (f32[44,256]{1,0:T(8,128)S(1)}, f32[44,256]{1,0:T(8,128)}, u32[]{:S(2)}) copy-start(f32[44,256]{1,0:T(8,128)} %param.8) | copy-start | bytes 135172
  114.8 9.1 %collective-permute-start.12 = (f32[64,256]{1,0:T(8,128)S(1)}, f32[64,256]{1,0:T(8,128)S(1)}, u32[]{:S(2)}, u32[]{:S(2)}) collective-permute-start(f32[64,256]{1,0:T(8,128)S(1)} %get-tuple-element.12), channel_id=1, source_target_pairs={{32,0},{64,32},{96,64},{33,1},{65,33},{97,65},{34,2},{66,34},{98,6... | collective-permute-start | bytes 196616 | tf_op jit(solution)/shard_map/ppermute | solution.py:33
  116.1 7.8 %collective-permute-start.13 = (f32[64,256]{1,0:T(8,128)S(1)}, f32[64,256]{1,0:T(8,128)S(1)}, u32[]{:S(2)}, u32[]{:S(2)}) collective-permute-start(f32[64,256]{1,0:T(8,128)S(1)} %get-tuple-element.9), channel_id=1, source_target_pairs={{0,32},{32,64},{64,96},{1,33},{33,65},{65,97},{2,34},{34,66},{66,9... | collective-permute-start | bytes 196616 | tf_op jit(solution)/shard_map/ppermute | solution.py:33
  119.1 6.6 %collective-permute-start.14 = (f32[64,256]{1,0:T(8,128)S(1)}, f32[64,256]{1,0:T(8,128)S(1)}, u32[]{:S(2)}, u32[]{:S(2)}) collective-permute-start(f32[64,256]{1,0:T(8,128)S(1)} %get-tuple-element.11), channel_id=1, source_target_pairs={{0,31},{1,0},{2,1},{3,2},{4,3},{5,4},{6,5},{7,6},{8,7},{9,8},{10,9... | collective-permute-start | bytes 196616 | tf_op jit(solution)/shard_map/ppermute | solution.py:27
  123.9 10.0 %collective-permute-start.15 = (f32[64,256]{1,0:T(8,128)S(1)}, f32[64,256]{1,0:T(8,128)S(1)}, u32[]{:S(2)}, u32[]{:S(2)}) collective-permute-start(f32[64,256]{1,0:T(8,128)S(1)} %get-tuple-element.10), channel_id=1, source_target_pairs={{0,1},{1,2},{2,3},{3,4},{4,5},{5,6},{6,7},{7,8},{8,9},{9,10},{10,1... | collective-permute-start | bytes 196616 | tf_op jit(solution)/shard_map/ppermute | solution.py:27
where the time goes:
time: 137 us; the launch traced here: 136 us
  starting transfers between devices  35.7 us (26%)
  waiting for transfers between devices  33.3 us (24%)
  local copies, waits for them, and re-layouts  32.6 us (24%)
  matrix products  25.8 us (19%)
  other arithmetic  8.72 us (6%)
    dot_general x5, matrix products, render_block(): lax.dot_general(residual, basis, (((1,), (1,)), ((), ())), preferred_elem...  22.3 us
    ppermute x10, waiting for transfers between devices, from_behind(): lax.ppermute(shard, axis, [(i, (i + by) % size) for i in range(size)])  21.5 us
    ppermute x10, starting transfers between devices, from_behind(): lax.ppermute(shard, axis, [(i, (i + by) % size) for i in range(size)])  20.4 us
    scatter x1, local copies, waits for them, and re-layouts, local(): packets = jnp.zeros((offsets * capacity, width_k), jnp.bfloat16).at[dest_...  16.9 us
    ppermute x2, starting transfers between devices, with_halo(): lax.ppermute(lax.slice_in_dim(block, 0, width, axis=dim), axis, backward)  10.9 us
    ppermute x2, waiting for transfers between devices, with_halo(): lax.ppermute(lax.slice_in_dim(block, block.shape[dim] - width, None, axis...  7.92 us
    gather x1, local copies, waits for them, and re-layouts, local(): returned.reshape(offsets * capacity, width_k)[dest_row].astype(jnp.float32)  5.35 us
    ppermute x2, starting transfers between devices, passed_along(): lax.ppermute(value, axis, [(source, source + steps) for source in range(i...  4.33 us
  transfers between devices with their start and end apart: 16, of which 5 were waited for; matrix products, arithmetic and copies ran while one was open for 21% of the time, Pallas kernels for 0%

commit v1 on v0

v1 whole, which is shorter than its diff:
```python
import math

import jax
import jax.numpy as jnp
from jax import lax
from jax.experimental import pallas as pl
from jax.experimental.pallas import tpu as pltpu
from jax.sharding import PartitionSpec as P

HIGH = lax.Precision.HIGHEST
MESH = pl.DeviceIdType.MESH
F32, BF16 = jnp.float32, jnp.bfloat16


def dot(a, b, da, db, precision=None):
    return lax.dot_general(
        a, b, (((da,), (db,)), ((), ())), precision=precision, preferred_element_type=F32
    )


def kernel(
    params_ref, mixing_ref, blend_ref, ids_ref, owners_ref, basis_hbm, seen_hbm, out_ref,
    seen, basis, amps, sig, back_out, back_in, rim_out, rim_in, w_out, w_in,
    seen_sem, basis_sem, back_ssem, back_rsem, rim_ssem, rim_rsem, w_ssem, w_rsem,
):
    noff, cap, pix = seen.shape
    reach = noff // 2
    rows, top = owners_ref.shape
    border = ids_ref.shape[1]
    scale = 1.0 / math.sqrt(pix)
    nd, nr = lax.axis_size("dec"), lax.axis_size("ra")
    dec, ra = lax.axis_index("dec"), lax.axis_index("ra")

    def at_ra(step):
        return (dec, lax.rem(ra + step + nr, nr))

    def at_dec(step):
        return (lax.rem(dec + step + nd, nd), ra)

    def turn(step):
        return jnp.where(lax.rem(step, 2) == 0, step // 2, noff - 1 - step // 2)

    def seen_copy(j):
        return pltpu.make_async_copy(seen_hbm.at[j], seen.at[j], seen_sem.at[j])

    def back_copy(j, step):
        return pltpu.make_async_remote_copy(
            src_ref=back_out.at[j], dst_ref=back_in.at[j],
            send_sem=back_ssem.at[j], recv_sem=back_rsem.at[j],
            device_id=at_ra(step), device_id_type=MESH,
        )

    def rim_copy(slot, where):
        return pltpu.make_async_remote_copy(
            src_ref=rim_out, dst_ref=rim_in.at[slot],
            send_sem=rim_ssem.at[slot], recv_sem=rim_rsem.at[slot],
            device_id=where, device_id_type=MESH,
        )

    def w_copy(slot, where):
        return pltpu.make_async_remote_copy(
            src_ref=w_out.at[slot], dst_ref=w_in.at[slot],
            send_sem=w_ssem.at[slot], recv_sem=w_rsem.at[slot],
            device_id=where, device_id_type=MESH,
        )

    basis_copy = pltpu.make_async_copy(basis_hbm, basis, basis_sem)
    basis_copy.start()
    for j in (0, 4, 1, 3, 2):
        seen_copy(j).start()

    barrier = pltpu.get_barrier_semaphore()
    peers = [at_dec(1), at_dec(-1)]
    for step in range(1, reach + 1):
        peers += [at_ra(step), at_ra(-step)]
    for peer in peers:
        pl.semaphore_signal(barrier, inc=1, device_id=peer, device_id_type=MESH)

    logits = dot(params_ref[...], mixing_ref[...], 0, 0, HIGH)
    decay = jnp.exp(-jnp.abs(logits))
    amps[...] = jnp.maximum(logits, 0.0) + jnp.log1p(decay)
    sig[...] = jnp.where(logits >= 0, 1.0, decay) / (1.0 + decay)
    pick = (lax.broadcasted_iota(jnp.int32, (rows, border), 0) == ids_ref[...]).astype(F32)
    rim_out[...] = dot(pick, amps[...], 0, 0, HIGH)

    pl.semaphore_wait(barrier, len(peers))
    rim_copies = [
        rim_copy(0, at_dec(1)), rim_copy(1, at_dec(-1)), rim_copy(2, at_ra(1)), rim_copy(3, at_ra(-1)),
    ]
    for copy in rim_copies:
        copy.start()

    basis_copy.wait()

    def render(step, carry):
        j = turn(step)
        seen_copy(j).wait()
        back_out[j] = (dot(seen[j], basis[...], 1, 1) * scale).astype(BF16)
        return carry

    def render_and_send(step, carry):
        render(step, carry)
        j = turn(step)
        back_copy(j, reach - j).start()
        return carry

    lax.fori_loop(0, noff - 1, render_and_send, 0)
    render(noff - 1, 0)

    gram = dot(basis[...], basis[...], 1, 1)
    gram_hi = gram.astype(BF16)
    gram_lo = (gram - gram_hi.astype(F32)).astype(BF16)

    for copy in rim_copies:
        copy.wait_recv()
    light = jnp.zeros((border, amps.shape[1]), F32)
    masks = (dec > 0, dec < nd - 1, None, None)
    for side in range(4):
        part = dot(blend_ref[side], rim_in[side], 1, 0, HIGH)
        light = light + (part if masks[side] is None else jnp.where(masks[side], part, 0.0))
    sent = (amps[...] + dot(pick, light, 1, 0, HIGH)).astype(BF16)
    base = (dot(sent, gram_hi, 1, 0) + dot(sent, gram_lo, 1, 0)) * (top * scale)

    total = noff * (noff - 1) // 2
    missing = total - jnp.sum(owners_ref[...], axis=1, keepdims=True)
    lanes = lax.broadcasted_iota(jnp.int32, (rows, 128), 1)
    member = (missing != lanes).astype(F32).astype(BF16)
    earlier = (
        lax.broadcasted_iota(jnp.int32, (rows, rows), 1)
        < lax.broadcasted_iota(jnp.int32, (rows, rows), 0)
    ).astype(F32).astype(BF16)
    slots = dot(earlier, member, 1, 0).astype(jnp.int32)
    places = lax.broadcasted_iota(jnp.int32, (rows, cap), 1)

    def unpacked(j, block):
        slot = jnp.where(missing != j, slots[:, j : j + 1], -1)
        chosen = (slot == places).astype(F32).astype(BF16)
        return dot(chosen, block, 1, 0)

    grad = base - unpacked(reach, back_out[reach])
    for j in (0, 4, 1, 3):
        back_copy(j, reach - j).wait_recv()
        grad = grad - unpacked(j, back_in[j])

    rim_grad = dot(pick, grad, 0, 0, HIGH)
    w_copies = [
        w_copy(0, at_dec(-1)), w_copy(1, at_dec(1)), w_copy(2, at_ra(-1)), w_copy(3, at_ra(1)),
    ]
    for side in (2, 3, 0, 1):
        toward = dot(blend_ref[side], rim_grad, 0, 0, HIGH)
        slope = 1.0 - jnp.exp(-rim_in[side])
        w_out[side] = dot(mixing_ref[...], toward * slope, 1, 1, HIGH)
        w_copies[side].start()
    out = dot(mixing_ref[...], grad * sig[...], 1, 1, HIGH)
    for copy in w_copies:
        copy.wait_recv()
    w = (
        jnp.where(dec < nd - 1, w_in[0], 0.0) + jnp.where(dec > 0, w_in[1], 0.0) + w_in[2] + w_in[3]
    )
    out_ref[...] = out + dot(w, pick, 1, 1, HIGH)
    for copy in rim_copies + w_copies:
        copy.wait_send()
    for j in (0, 4, 1, 3):
        back_copy(j, reach - j).wait_send()


def local(params, mixing, basis, blend, border_ids, intersection, observed):
    p_size, rows = params.shape[1:]
    k = mixing.shape[1]
    noff, cap, pix = observed.shape[1:]
    border = border_ids.shape[1]
    vmem = pl.BlockSpec(memory_space=pltpu.VMEM)
    hbm = pl.BlockSpec(memory_space=pl.ANY)
    dma = pltpu.SemaphoreType.DMA
    out = pl.pallas_call(
        kernel,
        out_shape=jax.ShapeDtypeStruct((p_size, rows), F32),
        in_specs=[vmem] * 5 + [hbm] * 2,
        out_specs=vmem,
        scratch_shapes=[
            pltpu.VMEM((noff, cap, pix), BF16),
            pltpu.VMEM((k, pix), BF16),
            pltpu.VMEM((rows, k), F32),
            pltpu.VMEM((rows, k), F32),
            pltpu.VMEM((noff, cap, k), BF16),
            pltpu.VMEM((noff, cap, k), BF16),
            pltpu.VMEM((border, k), F32),
            pltpu.VMEM((4, border, k), F32),
            pltpu.VMEM((4, p_size, border), F32),
            pltpu.VMEM((4, p_size, border), F32),
            dma((noff,)), dma, dma((noff,)), dma((noff,)), dma((4,)), dma((4,)), dma((4,)), dma((4,)),
        ],
        compiler_params=pltpu.CompilerParams(
            collective_id=0, has_side_effects=True, vmem_limit_bytes=48 * 1024 * 1024
        ),
        name="tiles",
    )(params[0], mixing, blend[0], border_ids, intersection[0], basis, observed[0])
    return out[None]


def solution(mesh):
    in_specs = (
        P(("dec", "ra"), None, None),
        P(),
        P(),
        P(("dec", "ra"), None, None, None),
        P(("dec", "ra"), None),
        P(("dec", "ra"), None, None),
        P(("dec", "ra"), None, None, None),
    )
    out_specs = P(("dec", "ra"), None, None)
    return jax.shard_map(local, mesh=mesh, in_specs=in_specs, out_specs=out_specs, check_vma=False)
```

time: 137 us -> 41.3 us (0.30)
  starting transfers between devices: 35.7 us -> 0 us
  Pallas kernels: 0 us -> 34.5 us
  waiting for transfers between devices: 33.3 us -> 0 us
  local copies, waits for them, and re-layouts: 32.6 us -> 6.35 us
  matrix products: 25.8 us -> 0 us
  other arithmetic: 8.72 us -> 0 us
    ppermute x16 -> x0, starting transfers between devices: 35.7 us -> none  [the longest x10 20.4 us: from_behind(): lax.ppermute(shard, axis, [(i, (i + by) % size) for i in range(size)])]
    pallas_call x0 -> x1, Pallas kernels: none -> 34.5 us  [local(): pl.pallas_call(kernel, out_shape=jax.ShapeDtypeStruct((p_size, rows), F32...]
    ppermute x16 -> x0, waiting for transfers between devices: 33.3 us -> none  [the longest x10 21.5 us: from_behind(): lax.ppermute(shard, axis, [(i, (i + by) % size) for i in range(size)])]
    dot_general x8 -> x0, matrix products: 25.5 us -> none  [the longest x5 22.3 us: render_block(): lax.dot_general(residual, basis, (((1,), (1,)), ((), ())), preferred_elem...]
    scatter x1 -> x0, local copies, waits for them, and re-layouts: 16.9 us -> none  [local(): packets = jnp.zeros((offsets * capacity, width_k), jnp.bfloat16).at[dest_...]
    gather x3 -> x0, local copies, waits for them, and re-layouts: 6.78 us -> none  [the longest x1 5.35 us: local(): returned.reshape(offsets * capacity, width_k)[dest_row].astype(jnp.float32)]
    unnamed x18 -> x10, local copies, waits for them, and re-layouts: 2.75 us -> 5.65 us
    convert_element_type x1 -> x0, local copies, waits for them, and re-layouts: 2.65 us -> none  [local(): returned.reshape(offsets * capacity, width_k)[dest_row].astype(jnp.float32)]
  transfers between devices with their start and end apart: 16 -> 0, of which waited for: 5 -> 0; matrix products, arithmetic and copies ran while one was open for 21% -> 0% of each run, Pallas kernels for 0% -> 0%
where the time goes in v1:
time: 41.3 us; the launch traced here: 40.9 us
  Pallas kernels  34.5 us (84%)
  local copies, waits for them, and re-layouts  6.35 us (15%)
    pallas_call x1, Pallas kernels, local(): pl.pallas_call(kernel, out_shape=jax.ShapeDtypeStruct((p_size, rows), F32...  34.5 us
    unnamed x10, local copies, waits for them, and re-layouts  5.65 us

profile of v1, /device:TPU:0, one launch (start us, length us, event | category | flops | bytes accessed | tf_op | source)
XLA Modules:
  0.0 40.9 jit_solution(17459833438668217276)
XLA Ops:
  0.0 0.9 %copy.12 = f32[1,44,384]{2,1,0:T(8,128)S(1)} copy(f32[1,44,384]{2,0,1:T(1,128)} %param.7) | data formatting | bytes 135168
  0.9 0.8 %copy.8 = s32[1,384,4]{2,1,0:T(8,128)S(1)} copy(s32[1,384,4]{1,2,0:T(4,128)} %param.12) | data formatting | bytes 12288 | tf_op args[5]
  1.7 0.0 copy-start
  1.7 1.6 %copy-done = bf16[256,4096]{1,0:T(8,128)(2,1)S(1)} copy-done((bf16[256,4096]{1,0:T(8,128)(2,1)S(1)}, bf16[256,4096]{1,0:T(8,128)(2,1)}, u32[]{:S(2)}) %copy-start) | copy-done | bytes 2097176
  3.3 0.0 copy-start.1
  3.3 0.9 %copy-done.1 = f32[1,4,64,64]{3,2,1,0:T(8,128)S(1)} copy-done((f32[1,4,64,64]{3,2,1,0:T(8,128)S(1)}, f32[1,4,64,64]{3,2,1,0:T(8,128)}, u32[]{:S(2)}) %copy-start.1) | copy-done | bytes 65560
  4.2 0.0 copy-start.2
  4.2 0.8 %copy-done.2 = f32[44,256]{1,0:T(8,128)S(1)} copy-done((f32[44,256]{1,0:T(8,128)S(1)}, f32[44,256]{1,0:T(8,128)}, u32[]{:S(2)}) %copy-start.2) | copy-done | bytes 45080
  5.0 0.0 copy-start.3
  5.0 0.7 %copy-done.3 = s32[1,64]{1,0:T(1,128)S(1)} copy-done((s32[1,64]{1,0:T(1,128)S(1)}, s32[1,64]{1,0:T(1,128)}, u32[]{:S(2)}) %copy-start.3) | copy-done | bytes 280
  5.7 34.5 %tiles.1 = f32[44,384]{1,0:T(8,128)S(1)} custom-call(f32[44,384]{1,0:T(8,128)S(1)} %bitcast.9, f32[44,256]{1,0:T(8,128)S(1)} %copy-done.2, f32[4,64,64]{2,1,0:T(8,128)S(1)} %bitcast.10, s32[1,64]{1,0:T(1,128)S(1)} %copy-done.3, s32[384,4]{1,0:T(8,128)S(1)} %bitcast.7, bf16[256,4096]{1,0:T(8,128)(2,1)S(1)} %copy-done, bf16[5,384,4096]{2,1,0:T(8,128)(2,1)} %bitcast.11), custom_call_target="tpu_custom_call" | custom-call | tf_op jit(solution)/shard_map/tiles/pallas_call | solution.py:175
  40.2 0.7 %copy.9 = f32[1,44,384]{2,0,1:T(1,128)} copy(f32[1,44,384]{2,1,0:T(8,128)S(1)} %bitcast.8) | data formatting | bytes 135168 | tf_op jit(solution)/shard_map/broadcast_in_dim | solution.py:198
Async XLA Ops:
  1.7 1.6 %copy-start = (bf16[256,4096]{1,0:T(8,128)(2,1)S(1)}, bf16[256,4096]{1,0:T(8,128)(2,1)}, u32[]{:S(2)}) copy-start(bf16[256,4096]{1,0:T(8,128)(2,1)} %basis_hbm.1) | copy-start | bytes 6291460
  3.3 0.9 %copy-start.1 = (f32[1,4,64,64]{3,2,1,0:T(8,128)S(1)}, f32[1,4,64,64]{3,2,1,0:T(8,128)}, u32[]{:S(2)}) copy-start(f32[1,4,64,64]{3,2,1,0:T(8,128)} %param.10) | copy-start | bytes 196612
  4.2 0.8 %copy-start.2 = (f32[44,256]{1,0:T(8,128)S(1)}, f32[44,256]{1,0:T(8,128)}, u32[]{:S(2)}) copy-start(f32[44,256]{1,0:T(8,128)} %mixing_ref.1) | copy-start | bytes 135172
  5.0 0.7 %copy-start.3 = (s32[1,64]{1,0:T(1,128)S(1)}, s32[1,64]{1,0:T(1,128)}, u32[]{:S(2)}) copy-start(s32[1,64]{1,0:T(1,128)} %ids_ref.1) | copy-start | bytes 772

commit v2 on v1

v2 whole, which is shorter than its diff:
```python
import math

import jax
import jax.numpy as jnp
from jax import lax
from jax.experimental import pallas as pl
from jax.experimental.pallas import tpu as pltpu
from jax.sharding import PartitionSpec as P

HIGH = lax.Precision.HIGHEST
MESH = pl.DeviceIdType.MESH
F32, BF16 = jnp.float32, jnp.bfloat16


def dot(a, b, da, db, precision=None):
    return lax.dot_general(
        a, b, (((da,), (db,)), ((), ())), precision=precision, preferred_element_type=F32
    )


def halves(x):
    high = x.astype(BF16)
    return high, (x - high.astype(F32)).astype(BF16)


def onehot(hit):
    return hit.astype(F32).astype(BF16)


def kernel(
    params_hbm, mixing_hbm, blend_hbm, ids_hbm, owners_hbm, basis_hbm, seen_hbm, out_ref,
    params_ref, mixing_ref, blend_ref, ids_ref, owners_ref, mix2, fwd_params, fwd_slots,
    seen, basis, packed, placed, q_out, q_in, z_out, z_in, rim_out, rim_in, w_out, w_in,
    in_sem, seen_sem, basis_sem, slots_ssem, slots_rsem, params_ssem, params_rsem,
    q_ssem, q_rsem, z_ssem, z_rsem, rim_ssem, rim_rsem, w_ssem, w_rsem,
):
    noff, cap, pix = seen.shape
    mid = noff // 2
    top, rows = owners_ref.shape
    border = ids_ref.shape[1]
    p_size = params_ref.shape[0]
    half = mix2.shape[0] // 2
    scale = 1.0 / math.sqrt(pix)
    share = top * scale
    nd, nr = lax.axis_size("dec"), lax.axis_size("ra")
    dec, ra = lax.axis_index("dec"), lax.axis_index("ra")
    others = [j for j in range(noff) if j != mid]

    def at_ra(step):
        return (dec, lax.rem(ra + step + nr, nr))

    def at_dec(step):
        return (lax.rem(dec + step + nd, nd), ra)

    def turn(step):
        return jnp.where(step < mid, step, jnp.where(step < noff - 1, step + 1, mid))

    def seen_copy(j):
        return pltpu.make_async_copy(seen_hbm.at[j], seen.at[j], seen_sem.at[j])

    def remote(src, dst, ssem, rsem, where):
        return pltpu.make_async_remote_copy(
            src_ref=src, dst_ref=dst, send_sem=ssem, recv_sem=rsem,
            device_id=where, device_id_type=MESH,
        )

    def slots_copy(j):
        return remote(
            fwd_slots.at[mid], fwd_slots.at[j], slots_ssem.at[j], slots_rsem.at[j], at_ra(j - mid)
        )

    def params_copy(j):
        return remote(
            fwd_params.at[mid], fwd_params.at[j], params_ssem.at[j], params_rsem.at[j], at_ra(j - mid)
        )

    def q_copy(j):
        return remote(q_out.at[j], q_in.at[j], q_ssem.at[j], q_rsem.at[j], at_ra(mid - j))

    def z_copy(j):
        return remote(z_out.at[j], z_in.at[j], z_ssem.at[j], z_rsem.at[j], at_ra(mid - j))

    def mixed(x, full=True):
        high, low = halves(x)
        both = dot(mix2[...], high, 1, 1)
        out = both[:p_size] + both[half : half + p_size]
        return out + dot(mix2[:half], low, 1, 1)[:p_size] if full else out

    in_copies = [
        pltpu.make_async_copy(src, dst, in_sem.at[n])
        for n, (src, dst) in enumerate((
            (ids_hbm, ids_ref), (owners_hbm, owners_ref), (params_hbm.at[:, 0, :], params_ref),
            (mixing_hbm, mixing_ref), (blend_hbm, blend_ref),
        ))
    ]
    for copy in in_copies:
        copy.start()
    basis_copy = pltpu.make_async_copy(basis_hbm, basis, basis_sem)
    basis_copy.start()
    seen_copy(0).start()

    barrier = pltpu.get_barrier_semaphore()
    peers = [at_dec(1), at_dec(-1)] + [at_ra(j - mid) for j in others]
    for peer in peers:
        pl.semaphore_signal(barrier, inc=1, device_id=peer, device_id_type=MESH)

    earlier = onehot(
        lax.broadcasted_iota(jnp.int32, (rows, rows), 0)
        < lax.broadcasted_iota(jnp.int32, (rows, rows), 1)
    )
    mix2[...] = jnp.zeros_like(mix2)
    for copy in in_copies:
        copy.wait()
    seen_copy(1).start()
    pick = onehot(lax.broadcasted_iota(jnp.int32, (rows, border), 0) == ids_ref[...])
    spare = noff * (noff - 1) // 2 - jnp.sum(owners_ref[...], axis=0, keepdims=True)
    member = spare != lax.broadcasted_iota(jnp.int32, (8, rows), 0)
    slots = jnp.where(member, dot(onehot(member), earlier, 1, 0), -1.0)
    slots_hi, slots_lo = halves(slots)
    fwd_slots[mid, :, :rows] = slots
    fwd_slots[mid, :, rows : rows + border] = dot(slots_hi, pick, 1, 0) + dot(slots_lo, pick, 1, 0)
    fwd_slots[mid, :, rows + border :] = jnp.full((8, fwd_slots.shape[2] - rows - border), -1.0, F32)
    params = params_ref[...]
    mixing = mixing_ref[...]
    mix_hi, mix_lo = halves(mixing)
    mix2[:p_size] = mix_hi
    mix2[half : half + p_size] = mix_lo
    fwd_params[mid] = params.astype(BF16)
    rim_params = dot(params, pick.astype(F32), 1, 0, HIGH)
    rim_logits = dot(rim_params, mixing, 0, 0, HIGH)
    rim_decay = jnp.exp(-jnp.abs(rim_logits))
    rim_out[...] = jnp.maximum(rim_logits, 0.0) + jnp.log1p(rim_decay)

    pl.semaphore_wait(barrier, len(peers))
    for j in others:
        slots_copy(j).start()
    for j in others:
        params_copy(j).start()
    rim_copies = [
        remote(rim_out, rim_in.at[slot], rim_ssem.at[slot], rim_rsem.at[slot], where)
        for slot, where in enumerate((at_dec(1), at_dec(-1), at_ra(1), at_ra(-1)))
    ]
    for copy in rim_copies:
        copy.start()

    basis_copy.wait()

    def render(step, carry):
        j = turn(step)
        seen_copy(j).wait()

        @pl.when(step + 2 < noff)
        def _():
            seen_copy(turn(step + 2)).start()

        packed[j] = (dot(seen[j], basis[...], 1, 1) * scale).astype(BF16)
        return carry

    lax.fori_loop(0, noff, render, 0)

    places = lax.broadcasted_iota(jnp.int32, (rows + border, cap), 1).astype(F32)

    def place(j):
        column = fwd_slots[j].T[: rows + border, j : j + 1]
        block = dot(onehot(column == places), packed[j], 1, 0)
        return block[:rows], block[rows:]

    for j in others:
        slots_copy(j).wait_recv()
        block, q = place(j)
        q_out[j] = q.astype(BF16)
        q_copy(j).start()
        placed[j] = block.astype(BF16)

    for j in others:
        params_copy(j).wait_recv()
        slope_in = dot(fwd_params[j], mix2[:p_size], 0, 0)
        z = mixed(placed[j].astype(F32) / (1.0 + jnp.exp(-slope_in)), False)
        z_out[j] = z.astype(BF16)
        z_copy(j).start()

    gram_hi, gram_lo = halves(dot(basis[...], basis[...], 1, 1))

    def through_gram(x):
        return (dot(x, gram_hi, 1, 0) + dot(x, gram_lo, 1, 0)) * share

    block_own, q_own = place(mid)
    logits = dot(params, mixing, 0, 0, HIGH)
    decay = jnp.exp(-jnp.abs(logits))
    amps = jnp.maximum(logits, 0.0) + jnp.log1p(decay)
    slope = jnp.where(logits >= 0, 1.0, decay) / (1.0 + decay)
    out = mixed((through_gram(amps.astype(BF16)) - block_own) * slope)

    for copy in rim_copies:
        copy.wait_recv()
    masks = (dec > 0, dec < nd - 1, None, None)
    light = jnp.zeros_like(rim_out)
    for side in range(4):
        part = dot(blend_ref[side], rim_in[side], 1, 0, HIGH)
        light = light + (part if masks[side] is None else jnp.where(masks[side], part, 0.0))
    rim_before = through_gram(rim_out[...].astype(BF16))
    rim_grad = through_gram((rim_out[...] + light).astype(BF16))
    rim_slope = jnp.where(rim_logits >= 0, 1.0, rim_decay) / (1.0 + rim_decay)
    w = mixed((rim_grad - rim_before) * rim_slope)
    rim_grad = rim_grad - q_own
    slopes = [1.0 - jnp.exp(-rim_in[side]) for side in range(4)]

    for j in others:
        q_copy(j).wait_recv()
        rim_grad = rim_grad - q_in[j].astype(F32)

    w_copies = [
        remote(w_out.at[side], w_in.at[side], w_ssem.at[side], w_rsem.at[side], where)
        for side, where in enumerate((at_dec(-1), at_dec(1), at_ra(-1), at_ra(1)))
    ]
    for side in (2, 3, 0, 1):
        toward = dot(blend_ref[side], rim_grad, 0, 0, HIGH)
        w_out[side] = mixed(toward * slopes[side])
        w_copies[side].start()

    for j in others:
        z_copy(j).wait_recv()
        out = out - z_in[j].astype(F32)

    for copy in w_copies:
        copy.wait_recv()
    w = w + (
        jnp.where(dec < nd - 1, w_in[0], 0.0) + jnp.where(dec > 0, w_in[1], 0.0) + w_in[2] + w_in[3]
    )
    w_hi, w_lo = halves(w)
    out_ref[:, 0, :] = out + (dot(w_hi, pick, 1, 1) + dot(w_lo, pick, 1, 1))
    for copy in rim_copies + w_copies:
        copy.wait_send()
    for j in others:
        for copy in (slots_copy(j), params_copy(j), q_copy(j), z_copy(j)):
            copy.wait_send()


def local(params, mixing, basis, blend, border_ids, intersection, observed):
    p_size, rows = params.shape[1:]
    k = mixing.shape[1]
    noff, cap, pix = observed.shape[1:]
    border = border_ids.shape[1]
    top = intersection.shape[2]
    half = -(-p_size // 16) * 16
    wide = -(-(rows + border) // 128) * 128
    hbm = pl.BlockSpec(memory_space=pltpu.HBM)
    vmem = pltpu.VMEM
    dma = pltpu.SemaphoreType.DMA
    out = pl.pallas_call(
        kernel,
        out_shape=jax.ShapeDtypeStruct((p_size, 1, rows), F32),
        in_specs=[hbm] * 7,
        out_specs=pl.BlockSpec(memory_space=pltpu.VMEM),
        scratch_shapes=[
            vmem((p_size, rows), F32),
            vmem((p_size, k), F32),
            vmem((4, border, border), F32),
            vmem((1, border), jnp.int32),
            vmem((top, rows), jnp.int32),
            vmem((2 * half, k), BF16),
            vmem((noff, p_size, rows), BF16),
            vmem((noff, 8, wide), F32),
            vmem((noff, cap, pix), BF16),
            vmem((k, pix), BF16),
            vmem((noff, cap, k), BF16),
            vmem((noff, rows, k), BF16),
            vmem((noff, border, k), BF16),
            vmem((noff, border, k), BF16),
            vmem((noff, p_size, rows), BF16),
            vmem((noff, p_size, rows), BF16),
            vmem((border, k), F32),
            vmem((4, border, k), F32),
            vmem((4, p_size, border), F32),
            vmem((4, p_size, border), F32),
            dma((5,)), dma((noff,)), dma,
            dma((noff,)), dma((noff,)), dma((noff,)), dma((noff,)),
            dma((noff,)), dma((noff,)), dma((noff,)), dma((noff,)),
            dma((4,)), dma((4,)), dma((4,)), dma((4,)),
        ],
        compiler_params=pltpu.CompilerParams(
            collective_id=0, has_side_effects=True, vmem_limit_bytes=67043328 - 80 * 1024
        ),
        name="tiles",
    )(jnp.swapaxes(params, 0, 1), mixing, blend[0], border_ids, intersection[0].T, basis, observed[0])
    return jnp.swapaxes(out, 0, 1)


def solution(mesh):
    in_specs = (
        P(("dec", "ra"), None, None),
        P(),
        P(),
        P(("dec", "ra"), None, None, None),
        P(("dec", "ra"), None),
        P(("dec", "ra"), None, None),
        P(("dec", "ra"), None, None, None),
    )
    out_specs = P(("dec", "ra"), None, None)
    return jax.shard_map(local, mesh=mesh, in_specs=in_specs, out_specs=out_specs, check_vma=False)
```

time: 41.3 us -> 32.9 us (0.80)
  local copies, waits for them, and re-layouts: 6.35 us -> 1.54 us
  Pallas kernels: 34.5 us -> 31.2 us
    unnamed x10 -> x1, local copies, waits for them, and re-layouts: 5.65 us -> 1.54 us
    pallas_call x1, Pallas kernels: 34.5 us -> 31.2 us  [local(): pl.pallas_call(kernel, out_shape=jax.ShapeDtypeStruct((p_size, 1, rows),...]
    broadcast_in_dim x1 -> x0, local copies, waits for them, and re-layouts: 0.7 us -> none  [local(): return out[None]]
where the time goes in v2:
time: 32.9 us; the launch traced here: 32.7 us
  Pallas kernels  31.2 us (95%)
  local copies, waits for them, and re-layouts  1.54 us (5%)
    pallas_call x1, Pallas kernels, local(): pl.pallas_call(kernel, out_shape=jax.ShapeDtypeStruct((p_size, 1, rows),...  31.2 us
    unnamed x1, local copies, waits for them, and re-layouts  1.54 us

profile of v2, /device:TPU:0, one launch (start us, length us, event | category | flops | bytes accessed | tf_op | source)
XLA Modules:
  0.0 32.7 jit_solution(9698754169538986378)
XLA Ops:
  0.0 31.2 %tiles.1 = f32[44,1,384]{2,1,0:T(1,128)} custom-call(f32[44,1,384]{2,1,0:T(1,128)} %bitcast.10, f32[44,256]{1,0:T(8,128)} %mixing_hbm.1, f32[4,64,64]{2,1,0:T(8,128)} %bitcast.9, s32[1,64]{1,0:T(1,128)} %ids_hbm.1, s32[4,384]{1,0:T(4,128)} %bitcast.11, bf16[256,4096]{1,0:T(8,128)(2,1)} %basis_hbm.1, bf16[5,384,4096]{2,1,0:T(8,128)(2,1)} %bitcast.7), custom_call_target="tpu_custom_call" | custom-call | tf_op jit(solution)/shard_map/tiles/pallas_call | solution.py:250
  31.2 1.5 %copy.9 = f32[1,44,384]{2,0,1:T(1,128)} copy(f32[1,44,384]{2,0,1:T(1,128)} %bitcast.8) | data formatting | bytes 135168

commit v3 on v2

--- a/solution.py
+++ b/solution.py
@@ -29,10 +29,12 @@
 
 def kernel(
     params_hbm, mixing_hbm, blend_hbm, ids_hbm, owners_hbm, basis_hbm, seen_hbm, out_ref,
-    params_ref, mixing_ref, blend_ref, ids_ref, owners_ref, mix2, fwd_params, fwd_slots,
+    params_ref, mixing_ref, blend_ref, ids_ref, owners_ref, mix2, fwd_params, slots_out, slots_in,
     seen, basis, packed, placed, q_out, q_in, z_out, z_in, rim_out, rim_in, w_out, w_in,
+    side_in, side_blend,
     in_sem, seen_sem, basis_sem, slots_ssem, slots_rsem, params_ssem, params_rsem,
     q_ssem, q_rsem, z_ssem, z_rsem, rim_ssem, rim_rsem, w_ssem, w_rsem,
+    side_ssem, side_rsem, blend_ssem, blend_rsem,
 ):
     noff, cap, pix = seen.shape
     mid = noff // 2
@@ -66,7 +68,7 @@
 
     def slots_copy(j):
         return remote(
-            fwd_slots.at[mid], fwd_slots.at[j], slots_ssem.at[j], slots_rsem.at[j], at_ra(j - mid)
+            slots_out.at[j], slots_in.at[j], slots_ssem.at[j], slots_rsem.at[j], at_ra(j - mid)
         )
 
     def params_copy(j):
@@ -79,6 +81,16 @@
 
     def z_copy(j):
         return remote(z_out.at[j], z_in.at[j], z_ssem.at[j], z_rsem.at[j], at_ra(mid - j))
+
+    def side_copy(n):
+        return remote(
+            q_out.at[(noff - 1, 0)[n]], side_in.at[n], side_ssem.at[n], side_rsem.at[n], at_ra((-1, 1)[n])
+        )
+
+    def blend_copy(n):
+        return remote(
+            blend_ref.at[3 - n], side_blend.at[n], blend_ssem.at[n], blend_rsem.at[n], at_ra((1, -1)[n])
+        )
 
     def mixed(x, full=True):
         high, low = halves(x)
@@ -108,18 +120,25 @@
         lax.broadcasted_iota(jnp.int32, (rows, rows), 0)
         < lax.broadcasted_iota(jnp.int32, (rows, rows), 1)
     )
-    mix2[...] = jnp.zeros_like(mix2)
-    for copy in in_copies:
+    for copy in in_copies[:2]:
         copy.wait()
-    seen_copy(1).start()
     pick = onehot(lax.broadcasted_iota(jnp.int32, (rows, border), 0) == ids_ref[...])
     spare = noff * (noff - 1) // 2 - jnp.sum(owners_ref[...], axis=0, keepdims=True)
     member = spare != lax.broadcasted_iota(jnp.int32, (8, rows), 0)
     slots = jnp.where(member, dot(onehot(member), earlier, 1, 0), -1.0)
     slots_hi, slots_lo = halves(slots)
-    fwd_slots[mid, :, :rows] = slots
-    fwd_slots[mid, :, rows : rows + border] = dot(slots_hi, pick, 1, 0) + dot(slots_lo, pick, 1, 0)
-    fwd_slots[mid, :, rows + border :] = jnp.full((8, fwd_slots.shape[2] - rows - border), -1.0, F32)
+    rim_slots = dot(slots_hi, pick, 1, 0) + dot(slots_lo, pick, 1, 0)
+    slots_out[...] = jnp.full(slots_out.shape, -1.0, F32)
+    for j in range(noff):
+        slots_out[j, :, :rows] = slots[j : j + 1]
+        slots_out[j, :, rows : rows + border] = rim_slots[j : j + 1]
+    pl.semaphore_wait(barrier, len(peers))
+    for j in others:
+        slots_copy(j).start()
+    mix2[...] = jnp.zeros_like(mix2)
+    for copy in in_copies[2:]:
+        copy.wait()
+    seen_copy(1).start()
     params = params_ref[...]
     mixing = mixing_ref[...]
     mix_hi, mix_lo = halves(mixing)
@@ -130,10 +149,6 @@
     rim_logits = dot(rim_params, mixing, 0, 0, HIGH)
     rim_decay = jnp.exp(-jnp.abs(rim_logits))
     rim_out[...] = jnp.maximum(rim_logits, 0.0) + jnp.log1p(rim_decay)
-
-    pl.semaphore_wait(barrier, len(peers))
-    for j in others:
-        slots_copy(j).start()
     for j in others:
         params_copy(j).start()
     rim_copies = [
@@ -142,6 +157,8 @@
     ]
     for copy in rim_copies:
         copy.start()
+    for n in range(2):
+        blend_copy(n).start()
 
     basis_copy.wait()
 
@@ -160,16 +177,21 @@
 
     places = lax.broadcasted_iota(jnp.int32, (rows + border, cap), 1).astype(F32)
 
-    def place(j):
-        column = fwd_slots[j].T[: rows + border, j : j + 1]
+    def place(row):
+        column = jnp.broadcast_to(row, (8, row.shape[1])).T[: rows + border, :1]
+        return column
+
+    def split(column, j):
         block = dot(onehot(column == places), packed[j], 1, 0)
         return block[:rows], block[rows:]
 
     for j in others:
         slots_copy(j).wait_recv()
-        block, q = place(j)
+        block, q = split(place(slots_in[j]), j)
         q_out[j] = q.astype(BF16)
         q_copy(j).start()
+        if j in (0, noff - 1):
+            side_copy(0 if j else 1).start()
         placed[j] = block.astype(BF16)
 
     for j in others:
@@ -184,39 +206,52 @@
     def through_gram(x):
         return (dot(x, gram_hi, 1, 0) + dot(x, gram_lo, 1, 0)) * share
 
-    block_own, q_own = place(mid)
+    block_own, q_own = split(place(slots_out[mid]), mid)
+
+    for copy in rim_copies:
+        copy.wait_recv()
+    masks = (dec > 0, dec < nd - 1, None, None)
+    light = jnp.zeros(rim_out.shape, F32)
+    for side in range(4):
+        part = dot(blend_ref[side], rim_in[side], 1, 0, HIGH)
+        light = light + (part if masks[side] is None else jnp.where(masks[side], part, 0.0))
+    rim_own = through_gram((rim_out[...] + light).astype(BF16))
+    rim_grad = rim_own - q_own
+    w_copies = [
+        remote(w_out.at[side], w_in.at[side], w_ssem.at[side], w_rsem.at[side], where)
+        for side, where in enumerate((at_dec(-1), at_dec(1), at_ra(-1), at_ra(1)))
+    ]
+
+    def tell(side, grad):
+        slope = 1.0 - jnp.exp(-rim_in[side])
+        w_out[side] = mixed(dot(blend_ref[side], grad, 0, 0, HIGH) * slope)
+        w_copies[side].start()
+
+    for j in range(mid):
+        q_copy(j).wait_recv()
+    from_west = q_in[0].astype(F32) + q_in[1].astype(F32)
+    tell(3, rim_grad - from_west)
+    for j in range(mid + 1, noff):
+        q_copy(j).wait_recv()
+    from_east = q_in[mid + 1].astype(F32) + q_in[noff - 1].astype(F32)
+    tell(2, rim_grad - from_east)
+    rim_grad = rim_grad - from_west - from_east
+    for side in range(2):
+        tell(side, rim_grad)
+
     logits = dot(params, mixing, 0, 0, HIGH)
     decay = jnp.exp(-jnp.abs(logits))
     amps = jnp.maximum(logits, 0.0) + jnp.log1p(decay)
     slope = jnp.where(logits >= 0, 1.0, decay) / (1.0 + decay)
     out = mixed((through_gram(amps.astype(BF16)) - block_own) * slope)
-
-    for copy in rim_copies:
-        copy.wait_recv()
-    masks = (dec > 0, dec < nd - 1, None, None)
-    light = jnp.zeros_like(rim_out)
-    for side in range(4):
-        part = dot(blend_ref[side], rim_in[side], 1, 0, HIGH)
-        light = light + (part if masks[side] is None else jnp.where(masks[side], part, 0.0))
-    rim_before = through_gram(rim_out[...].astype(BF16))
-    rim_grad = through_gram((rim_out[...] + light).astype(BF16))
     rim_slope = jnp.where(rim_logits >= 0, 1.0, rim_decay) / (1.0 + rim_decay)
-    w = mixed((rim_grad - rim_before) * rim_slope)
-    rim_grad = rim_grad - q_own
-    slopes = [1.0 - jnp.exp(-rim_in[side]) for side in range(4)]
-
-    for j in others:
-        q_copy(j).wait_recv()
-        rim_grad = rim_grad - q_in[j].astype(F32)
-
-    w_copies = [
-        remote(w_out.at[side], w_in.at[side], w_ssem.at[side], w_rsem.at[side], where)
-        for side, where in enumerate((at_dec(-1), at_dec(1), at_ra(-1), at_ra(1)))
-    ]
-    for side in (2, 3, 0, 1):
-        toward = dot(blend_ref[side], rim_grad, 0, 0, HIGH)
-        w_out[side] = mixed(toward * slopes[side])
-        w_copies[side].start()
+    gained = rim_own - through_gram(rim_out[...].astype(BF16))
+    for n in range(2):
+        blend_copy(n).wait_recv()
+        side_copy(n).wait_recv()
+        heard = q_out[(mid + 1, mid - 1)[n]].astype(F32) + side_in[n].astype(F32)
+        gained = gained - dot(side_blend[n], heard, 0, 0, HIGH)
+    w = mixed(gained * rim_slope)
 
     for j in others:
         z_copy(j).wait_recv()
@@ -234,6 +269,9 @@
     for j in others:
         for copy in (slots_copy(j), params_copy(j), q_copy(j), z_copy(j)):
             copy.wait_send()
+    for n in range(2):
+        side_copy(n).wait_send()
+        blend_copy(n).wait_send()
 
 
 def local(params, mixing, basis, blend, border_ids, intersection, observed):
@@ -260,7 +298,8 @@
             vmem((top, rows), jnp.int32),
             vmem((2 * half, k), BF16),
             vmem((noff, p_size, rows), BF16),
-            vmem((noff, 8, wide), F32),
+            vmem((noff, 1, wide), F32),
+            vmem((noff, 1, wide), F32),
             vmem((noff, cap, pix), BF16),
             vmem((k, pix), BF16),
             vmem((noff, cap, k), BF16),
@@ -273,16 +312,24 @@
             vmem((4, border, k), F32),
             vmem((4, p_size, border), F32),
             vmem((4, p_size, border), F32),
+            vmem((2, border, k), BF16),
+            vmem((2, border, border), F32),
             dma((5,)), dma((noff,)), dma,
             dma((noff,)), dma((noff,)), dma((noff,)), dma((noff,)),
             dma((noff,)), dma((noff,)), dma((noff,)), dma((noff,)),
             dma((4,)), dma((4,)), dma((4,)), dma((4,)),
+            dma((2,)), dma((2,)), dma((2,)), dma((2,)),
         ],
         compiler_params=pltpu.CompilerParams(
-            collective_id=0, has_side_effects=True, vmem_limit_bytes=67043328 - 80 * 1024
+            collective_id=0, has_side_effects=True, vmem_limit_bytes=48 * 1024 * 1024
         ),
         name="tiles",
-    )(jnp.swapaxes(params, 0, 1), mixing, blend[0], border_ids, intersection[0].T, basis, observed[0])
+    )(*[
+        pltpu.with_memory_space_constraint(x, pltpu.HBM)
+        for x in (
+            jnp.swapaxes(params, 0, 1), mixing, blend[0], border_ids, intersection[0].T, basis, observed[0],
+        )
+    ])
     return jnp.swapaxes(out, 0, 1)
 
 

time: 32.9 us -> 29.4 us (0.89)
  Pallas kernels: 31.2 us -> 28.4 us
  local copies, waits for them, and re-layouts: 1.54 us -> 0.63 us
    pallas_call x1, Pallas kernels: 31.2 us -> 28.4 us  [local(): pl.pallas_call(kernel, out_shape=jax.ShapeDtypeStruct((p_size, 1, rows),...]
    unnamed x1, local copies, waits for them, and re-layouts: 1.54 us -> 0.63 us
where the time goes in v3:
time: 29.4 us; the launch traced here: 29 us
  Pallas kernels  28.4 us (97%)
  local copies, waits for them, and re-layouts  0.63 us (2%)
    pallas_call x1, Pallas kernels, local(): pl.pallas_call(kernel, out_shape=jax.ShapeDtypeStruct((p_size, 1, rows),...  28.4 us
    unnamed x1, local copies, waits for them, and re-layouts  0.63 us

profile of v3, /device:TPU:0, one launch (start us, length us, event | category | flops | bytes accessed | tf_op | source)
XLA Modules:
  0.0 29.0 jit_solution(15799021463296726790)
XLA Ops:
  0.0 28.4 %tiles.1 = f32[44,1,384]{2,1,0:T(1,128)S(1)} custom-call(f32[44,1,384]{2,1,0:T(1,128)} %bitcast.10, f32[44,256]{1,0:T(8,128)} %mixing_hbm.1, f32[4,64,64]{2,1,0:T(8,128)} %bitcast.9, s32[1,64]{1,0:T(1,128)} %ids_hbm.1, s32[4,384]{1,0:T(4,128)} %bitcast.11, bf16[256,4096]{1,0:T(8,128)(2,1)} %basis_hbm.1, bf16[5,384,4096]{2,1,0:T(8,128)(2,1)} %bitcast.8), custom_call_target="tpu_custom_call" | custom-call | tf_op jit(solution)/shard_map/tiles/pallas_call | solution.py:288
  28.4 0.6 %copy.9 = f32[1,44,384]{2,0,1:T(1,128)} copy(f32[1,44,384]{2,0,1:T(1,128)S(1)} %bitcast.7) | data formatting | bytes 135168

commit v4 on v3

--- a/solution.py
+++ b/solution.py
@@ -194,13 +194,6 @@
             side_copy(0 if j else 1).start()
         placed[j] = block.astype(BF16)
 
-    for j in others:
-        params_copy(j).wait_recv()
-        slope_in = dot(fwd_params[j], mix2[:p_size], 0, 0)
-        z = mixed(placed[j].astype(F32) / (1.0 + jnp.exp(-slope_in)), False)
-        z_out[j] = z.astype(BF16)
-        z_copy(j).start()
-
     gram_hi, gram_lo = halves(dot(basis[...], basis[...], 1, 1))
 
     def through_gram(x):
@@ -227,6 +220,13 @@
         w_out[side] = mixed(dot(blend_ref[side], grad, 0, 0, HIGH) * slope)
         w_copies[side].start()
 
+    for j in others:
+        params_copy(j).wait_recv()
+        slope_in = dot(fwd_params[j], mix2[:p_size], 0, 0)
+        z = mixed(placed[j].astype(F32) / (1.0 + jnp.exp(-slope_in)), False)
+        z_out[j] = z.astype(BF16)
+        z_copy(j).start()
+
     for j in range(mid):
         q_copy(j).wait_recv()
     from_west = q_in[0].astype(F32) + q_in[1].astype(F32)
@@ -234,10 +234,9 @@
     for j in range(mid + 1, noff):
         q_copy(j).wait_recv()
     from_east = q_in[mid + 1].astype(F32) + q_in[noff - 1].astype(F32)
+    for side in range(2):
+        tell(side, rim_grad - from_west - from_east)
     tell(2, rim_grad - from_east)
-    rim_grad = rim_grad - from_west - from_east
-    for side in range(2):
-        tell(side, rim_grad)
 
     logits = dot(params, mixing, 0, 0, HIGH)
     decay = jnp.exp(-jnp.abs(logits))

time: 29.4 us -> 29.1 us (0.990)
  no operation moved by 1% of the time
where the time goes in v4:
time: 29.1 us; the launch traced here: 29 us
  Pallas kernels  28.3 us (97%)
  local copies, waits for them, and re-layouts  0.63 us (2%)
    pallas_call x1, Pallas kernels, local(): pl.pallas_call(kernel, out_shape=jax.ShapeDtypeStruct((p_size, 1, rows),...  28.3 us
    unnamed x1, local copies, waits for them, and re-layouts  0.63 us

profile of v4, /device:TPU:0, one launch (start us, length us, event | category | flops | bytes accessed | tf_op | source)
XLA Modules:
  0.0 29.0 jit_solution(12709610691286550818)
XLA Ops:
  0.0 28.3 %tiles.1 = f32[44,1,384]{2,1,0:T(1,128)S(1)} custom-call(f32[44,1,384]{2,1,0:T(1,128)} %bitcast.10, f32[44,256]{1,0:T(8,128)} %mixing_hbm.1, f32[4,64,64]{2,1,0:T(8,128)} %bitcast.9, s32[1,64]{1,0:T(1,128)} %ids_hbm.1, s32[4,384]{1,0:T(4,128)} %bitcast.11, bf16[256,4096]{1,0:T(8,128)(2,1)} %basis_hbm.1, bf16[5,384,4096]{2,1,0:T(8,128)(2,1)} %bitcast.8), custom_call_target="tpu_custom_call" | custom-call | tf_op jit(solution)/shard_map/tiles/pallas_call | solution.py:287
  28.3 0.6 %copy.9 = f32[1,44,384]{2,0,1:T(1,128)} copy(f32[1,44,384]{2,0,1:T(1,128)S(1)} %bitcast.7) | data formatting | bytes 135168
